TPU v7x, 512 devices: a whole 4x4x16 slice. The times are simulated.
512 devices in a mesh: samp: 64 (over z, y), hour: 8 (over x, core).
Axes of the slice: x: 4, y: 4, z: 16, core: 2. Of those that a mesh axis runs over, the one named last changes fastest.
Arguments:
- load_gap: float32 [3008, 4, 256], P('samp', None, 'hour'), may hold values from -21 to 21
- profiles: bfloat16 [4, 256, 131072], P(None, 'hour', 'samp'), may hold values from 0.019897461 to 0.3984375
- slot_of_sample: int32 [131072], P('samp'), may hold values from 0 to 1023, as said below
- slot_county: int32 [64, 1024], replicated, may hold values from 0 to 3007, as said below
Outputs:
- weight_step: float32 [4, 131072], P(None, ('samp', 'hour'))
- search_dir: float32 [4, 131072], P(None, ('samp', 'hour'))
- load_dir: float32 [3008, 4, 256], P('samp', None, 'hour')
Inputs may be any that keep to these rules, and one draw needn't show every extreme that they name: `slot_of_sample`: every slot 0 to 1023 of an index of samp is used by some sample of that index. `slot_county`: row d lists 1024 distinct counties in increasing order; county c is owned by index c // 47 of samp. At most 32 counties of a row have one owner; in every draw some owner has exactly 32 counties in every row.
All inputs are finite; a program needn't handle non-finite values.
Results may differ from a plain program's by a relative error of at most 0.00062.
Values sent between devices are 32-bit elements; how exact they have to be, the bound alone decides.
A program may use at most 64 MiB of HBM per device.

v0:
```python
import jax
import jax.numpy as jnp
from jax import lax
from jax.sharding import PartitionSpec as P

epsilon = 1e-06
PAD = 48


def two_pieces(x, axis):
    high = lax.reduce_precision(x, 8, 7)
    return jnp.concatenate([high, x - high], axis=axis).astype(jnp.bfloat16)


def local(load_gap, profiles, slot_of_sample, slot_county):
    owners = lax.axis_size("samp")
    hour_count = lax.axis_size("hour")
    owner_index = lax.axis_index("samp")
    hour_index = lax.axis_index("hour")
    use_count, hour_dev, samp_dev = profiles.shape
    per_owner = load_gap.shape[0]
    row_width = use_count * hour_dev
    share_len = samp_dev // hour_count
    space_count = float(per_owner * owners * row_width * hour_count)
    sample_count = float(use_count * samp_dev * owners)
    my_counties = lax.dynamic_index_in_dim(slot_county, owner_index, 0, keepdims=False)
    county = jnp.take(my_counties, slot_of_sample)
    place = county // per_owner * PAD + county % per_owner
    places = jnp.arange(owners * PAD, dtype=jnp.int32)
    onehot = (places[:, None] == place[None, :]).astype(jnp.bfloat16)
    wide = profiles.astype(jnp.float32)

    def padded(rows):
        return jnp.pad(rows, ((0, PAD - per_owner), (0, 0)))

    def backward(rows):
        everyone = lax.all_gather(padded(rows), "samp", tiled=True)
        square = jnp.sum(everyone * everyone)
        pieces = two_pieces(everyone, 1)
        spread = lax.dot_general(
            pieces, onehot, (((0,), (0,)), ((), ())), preferred_element_type=jnp.float32
        )
        spread = (spread[:row_width] + spread[row_width:]).reshape(use_count, hour_dev, samp_dev)
        partial = jnp.sum(wide * spread, axis=1)
        extra = jnp.zeros((1, samp_dev), jnp.float32).at[0, 0].set(square)
        total = lax.psum(jnp.concatenate([partial, extra], axis=0), "hour")
        return (total[:use_count], total[use_count, 0])

    def my_share(x):
        return lax.dynamic_slice_in_dim(x, hour_index * share_len, share_len, 1)

    gap_rows = load_gap.reshape(per_owner, row_width)
    plain, gap_total = backward(gap_rows)
    beta_one = jnp.sqrt(gap_total / space_count + epsilon)
    image = plain / beta_one
    weighted = (wide * image[:, None, :]).reshape(row_width, samp_dev)
    sums = lax.dot_general(
        onehot,
        two_pieces(weighted, 0),
        (((1,), (1,)), ((), ())),
        preferred_element_type=jnp.float32,
    )
    sums = (sums[:, :row_width] + sums[:, row_width:]).reshape(owners, PAD, row_width)
    mine = jnp.sum(image * image)
    row = jnp.arange(PAD, dtype=jnp.int32)[None, :, None]
    sums = jnp.where(row == per_owner, mine, sums).reshape(owners * PAD, row_width)
    owned = lax.psum_scatter(sums, "samp", scatter_dimension=0, tiled=True)
    alpha_one = jnp.sqrt(owned[per_owner, 0] / sample_count + epsilon)
    mismatch = owned[:per_owner] / alpha_one - alpha_one / beta_one * gap_rows
    back, mismatch_total = backward(mismatch)
    beta_two = jnp.sqrt(mismatch_total / space_count + epsilon)
    load_dir = mismatch / beta_two
    vector_one = image / alpha_one
    image_two = back / beta_two - beta_two * vector_one
    second_total = lax.psum(jnp.sum(image_two * image_two), "samp")
    alpha_two = jnp.sqrt(second_total / sample_count + epsilon)
    rho_value = jnp.sqrt(alpha_one * alpha_one + beta_two * beta_two)
    cosine = alpha_one / rho_value
    sine = beta_two / rho_value
    vector_share = my_share(vector_one)
    weight_step = cosine * beta_one / rho_value * vector_share
    search_dir = my_share(image_two) / alpha_two - sine * alpha_two / rho_value * vector_share
    return (weight_step, search_dir, load_dir.reshape(per_owner, use_count, hour_dev))


def solution(mesh):
    return jax.shard_map(
        local,
        mesh=mesh,
        in_specs=(P("samp", None, "hour"), P(None, "hour", "samp"), P("samp"), P()),
        out_specs=(P(None, ("samp", "hour")), P(None, ("samp", "hour")), P("samp", None, "hour")),
        check_vma=False,
    )
```

profile of v0, /device:TPU:8, one launch (start us, length us, event | category | flops | bytes accessed | tf_op | source)
XLA Modules:
  0.0 1211.6 jit_solution(9387377253845586838)
XLA Ops:
  7.2 0.0 copy-start
  7.2 0.0 all-gather.3.cloned.1.call-start
  7.2 0.9 copy.11
  8.2 0.6 pad.18
  8.8 0.0 all-gather.3.cloned.1.call-update
  8.8 0.0 reduce-scatter.2.cloned.1.call-start
  8.9 0.1 broadcast_in_dim.29
  9.0 0.0 copy-done
  9.0 0.7 fusion.25
  9.7 0.0 copy-start.2
  9.7 8.6 gather_fusion
  18.3 0.6 compare_reduce_fusion
  19.0 0.0 copy-done.2
  19.0 136.3 %all-gather.3.cloned.1.call-done = f32[3072,128]{1,0:T(8,128)} async-done(((f32[48,128]{1,0:T(8,128)}), f32[3072,128]{1,0:T(8,128)}) %all-gather.3.cloned.1.call-update) | async-done | bytes 1572880 | tf_op jit(solution)/shard_map/all_gather | solution.py:37
  155.2 2.4 reduce-precision_convert_fusion.1
  159.0 0.0 copy-start.1
  159.0 4.9 fusion.2
  163.9 0.0 copy-done.1
  163.9 0.3 fusion.16
  164.2 24.1 %psum.21 = f32[5,2048]{1,0:T(8,128)S(1)} all-reduce(f32[5,2048]{1,0:T(8,128)S(1)} %select_maximum_fusion.1), channel_id=1, replica_groups=mesh['samp'=64,'hour'=8] {'hour'}, use_global_device_ids=true, to_apply=%region_3.4 | all-reduce | flops 10240 | bytes 81920 | tf_op jit(solution)/shard_map/psum | solution.py:46
  188.4 0.5 slice.85
  189.6 0.6 multiply_reduce_fusion.3
  190.2 0.1 convert_multiply_fusion.1
  190.3 0.1 reduce-precision_convert_fusion.2
  190.5 4.9 fusion.1
  195.4 3.1 fusion.8
  198.5 0.0 reduce-scatter.2.cloned.1.call-update
  198.5 0.0 all-gather.5.cloned.1.call-start
  198.6 687.6 %reduce-scatter.2.cloned.1.call-done = f32[48,128]{1,0:T(8,128)} async-done(((f32[3072,128]{1,0:T(8,128)}), f32[48,128]{1,0:T(8,128)}) %reduce-scatter.2.cloned.1.call-update) | async-done | bytes 24592 | tf_op jit(solution)/shard_map/reduce_scatter | solution.py:67
  886.2 1.2 slice.88
  888.1 0.7 fusion.21
  888.9 0.6 pad.19
  889.5 0.0 all-gather.5.cloned.1.call-update
  889.5 138.2 %all-gather.5.cloned.1.call-done = f32[3072,128]{1,0:T(8,128)} async-done(((f32[48,128]{1,0:T(8,128)}), f32[3072,128]{1,0:T(8,128)}) %all-gather.5.cloned.1.call-update) | async-done | bytes 1572880 | tf_op jit(solution)/shard_map/all_gather | solution.py:37
  1027.7 2.4 reduce-precision_convert_fusion
  1031.4 4.9 fusion
  1036.4 0.3 fusion.17
  1036.7 23.9 %psum.22 = f32[5,2048]{1,0:T(8,128)S(1)} all-reduce(f32[5,2048]{1,0:T(8,128)S(1)} %select_maximum_fusion), channel_id=1, replica_groups=mesh['samp'=64,'hour'=8] {'hour'}, use_global_device_ids=true, to_apply=%region_8.9 | all-reduce | flops 10240 | bytes 81920 | tf_op jit(solution)/shard_map/psum | solution.py:46
  1060.6 0.5 slice.92
  1062.0 0.6 multiply_reduce_fusion.2
  1062.6 140.4 %psum.23 = f32[]{:T(128)} all-reduce(f32[]{:T(128)} %get-tuple-element.33), channel_id=1, replica_groups=mesh['samp'=64,'hour'=8] {'samp'}, use_global_device_ids=true, to_apply=%region_10.11 | all-reduce | flops 1 | bytes 8 | tf_op jit(solution)/shard_map/psum | solution.py:75
  1203.7 0.7 copy.12
  1204.5 0.6 divide_subtract_fusion.1
  (7 shorter events, 0.1 us)
Async XLA Ops:
  7.2 1.8 copy-start
  7.2 148.1 %all-gather.3.cloned.1.call-start = ((), (), s32[]{:S(2)}) async-start(), calls=%async_computation.1 | async-start | bytes 1597440 | tf_op jit(solution)/shard_map/all_gather | solution.py:37
  8.8 877.4 %reduce-scatter.2.cloned.1.call-start = ((), (), s32[]{:S(2)}) async-start(), calls=%async_computation.2 | async-start | bytes 1597440 | tf_op jit(solution)/shard_map/reduce_scatter | solution.py:67
  9.7 9.2 copy-start.2
  159.0 5.0 copy-start.1
  198.5 829.1 %all-gather.5.cloned.1.call-start = ((), (), s32[]{:S(2)}) async-start(), calls=%async_computation.3 | async-start | bytes 1597440 | tf_op jit(solution)/shard_map/all_gather | solution.py:37
Sparse Core Ops, SparseCore 0:
  11.5 143.6 all-gather.2
  198.7 687.4 reduce-scatter.1
  890.1 137.4 all-gather.4
where the time goes:
time: 1210 us
  waiting for transfers between devices  962 us (80%)
  blocking collectives  188 us (16%)
  between operations  19.5 us (2%)
  matrix products  14.8 us (1%)
  local copies, waits for them, and re-layouts  13.8 us (1%)
  other arithmetic  12.8 us (1%)
    reduce_scatter x1, waiting for transfers between devices, local(): owned = lax.psum_scatter(sums, 'samp', scatter_dimension=0, tiled=True)  688 us
    all_gather x2, waiting for transfers between devices, backward(): everyone = lax.all_gather(padded(rows), 'samp', tiled=True)  274 us
    psum x1, blocking collectives, local(): second_total = lax.psum(jnp.sum(image_two * image_two), 'samp')  140 us
    psum x2, blocking collectives, backward(): total = lax.psum(jnp.concatenate([partial, extra], axis=0), 'hour')  48.1 us
  transfers between devices with their start and end apart: 3, of which 3 were waited for; matrix products, arithmetic and copies ran while one was open for 1% of the time, Pallas kernels for 0%

commit v1 on v0

--- a/solution.py
+++ b/solution.py
@@ -34,7 +34,9 @@
         return jnp.pad(rows, ((0, PAD - per_owner), (0, 0)))
 
     def backward(rows):
-        everyone = lax.all_gather(padded(rows), "samp", tiled=True)
+        everyone = jnp.concatenate(
+            lax.all_to_all(jnp.stack([padded(rows)] * lax.axis_size("samp")), "samp", 0, 0), axis=0
+        )
         square = jnp.sum(everyone * everyone)
         pieces = two_pieces(everyone, 1)
         spread = lax.dot_general(

time: 1210 us -> 1100 us (0.909)
  waiting for transfers between devices: 962 us -> 817 us
  starting transfers between devices: 0.12 us -> 31.3 us
    all_gather x2 -> x0, waiting for transfers between devices: 274 us -> none  [backward(): everyone = lax.all_gather(padded(rows), 'samp', tiled=True)]
    all_to_all x0 -> x2, waiting for transfers between devices: none -> 134 us  [backward(): lax.all_to_all(jnp.stack([padded(rows)] * lax.axis_size('samp')), 'samp',...]
    all_to_all x0 -> x2, starting transfers between devices: none -> 31.3 us  [backward(): lax.all_to_all(jnp.stack([padded(rows)] * lax.axis_size('samp')), 'samp',...]
where the time goes in v1:
time: 1100 us
  waiting for transfers between devices  817 us (74%)
  blocking collectives  187 us (17%)
  starting transfers between devices  31.3 us (3%)
  between operations  19.9 us (2%)
  local copies, waits for them, and re-layouts  15.1 us (1%)
  matrix products  14.8 us (1%)
    reduce_scatter x1, waiting for transfers between devices, local(): owned = lax.psum_scatter(sums, 'samp', scatter_dimension=0, tiled=True)  683 us
    psum x1, blocking collectives, local(): second_total = lax.psum(jnp.sum(image_two * image_two), 'samp')  139 us
    all_to_all x2, waiting for transfers between devices, backward(): lax.all_to_all(jnp.stack([padded(rows)] * lax.axis_size('samp')), 'samp',...  134 us
    psum x2, blocking collectives, backward(): total = lax.psum(jnp.concatenate([partial, extra], axis=0), 'hour')  48.1 us
    all_to_all x2, starting transfers between devices, backward(): lax.all_to_all(jnp.stack([padded(rows)] * lax.axis_size('samp')), 'samp',...  31.3 us
  transfers between devices with their start and end apart: 3, of which 3 were waited for; matrix products, arithmetic and copies ran while one was open for 1% of the time, Pallas kernels for 0%

profile of v1, /device:TPU:8, one launch (start us, length us, event | category | flops | bytes accessed | tf_op | source)
XLA Modules:
  0.0 1095.7 jit_solution(9769979153117005803)
XLA Ops:
  7.2 0.0 copy-start
  7.2 1.0 copy.13
  8.2 0.0 copy-start.2
  8.2 1.3 stack.4
  9.4 18.7 %all-to-all-start = ((f32[64,48,128]{2,1,0:T(8,128)}), f32[64,48,128]{2,1,0:T(8,128)S(1)}, u32[]{:S(2)}, u32[]{:S(2)}) async-start(f32[64,48,128]{2,1,0:T(8,128)} %stack.4), calls=%async_computation | async-start | bytes 3145728 | tf_op jit(solution)/shard_map/all_to_all | solution.py:38
  28.2 0.0 reduce-scatter.2.cloned.1.call-start
  28.2 0.1 broadcast_in_dim.29
  28.3 0.0 copy-done
  28.3 0.0 copy-done.2
  28.4 8.6 gather_fusion
  37.0 0.6 compare_reduce_fusion
  37.6 68.2 %all-to-all-done = f32[64,48,128]{2,1,0:T(8,128)S(1)} async-done(((f32[64,48,128]{2,1,0:T(8,128)}), f32[64,48,128]{2,1,0:T(8,128)S(1)}, u32[]{:S(2)}, u32[]{:S(2)}) %all-to-all-start) | async-done | bytes 1572896 | tf_op jit(solution)/shard_map/all_to_all | solution.py:38
  105.8 1.0 multiply_reduce_fusion.1
  108.1 0.2 reduce-precision_convert_fusion.1
  108.4 0.0 copy-start.1
  108.4 4.9 fusion.2
  113.3 0.0 copy-done.1
  113.3 0.3 fusion.16
  113.6 24.1 %psum.21 = f32[5,2048]{1,0:T(8,128)S(1)} all-reduce(f32[5,2048]{1,0:T(8,128)S(1)} %select_maximum_fusion.1), channel_id=1, replica_groups=mesh['samp'=64,'hour'=8] {'hour'}, use_global_device_ids=true, to_apply=%region_3.4 | all-reduce | flops 10240 | bytes 81920 | tf_op jit(solution)/shard_map/psum | solution.py:48
  137.7 0.5 slice.85
  139.0 0.6 multiply_reduce_fusion.3
  139.6 0.1 convert_multiply_fusion.1
  139.7 0.1 reduce-precision_convert_fusion.2
  139.8 4.9 fusion.1
  144.8 3.1 fusion.8
  147.9 0.0 reduce-scatter.2.cloned.1.call-update
  147.9 683.4 %reduce-scatter.2.cloned.1.call-done = f32[48,128]{1,0:T(8,128)} async-done(((f32[3072,128]{1,0:T(8,128)}), f32[48,128]{1,0:T(8,128)}) %reduce-scatter.2.cloned.1.call-update) | async-done | bytes 24592 | tf_op jit(solution)/shard_map/reduce_scatter | solution.py:69
  831.3 1.2 slice.88
  833.3 0.7 fusion.21
  834.0 1.3 stack.5
  835.3 12.5 %all-to-all-start.1 = ((f32[64,48,128]{2,1,0:T(8,128)}), f32[64,48,128]{2,1,0:T(8,128)S(1)}, u32[]{:S(2)}, u32[]{:S(2)}) async-start(f32[64,48,128]{2,1,0:T(8,128)} %stack.5), calls=%async_computation.2 | async-start | bytes 3145728 | tf_op jit(solution)/shard_map/all_to_all | solution.py:38
  847.8 65.9 %all-to-all-done.1 = f32[64,48,128]{2,1,0:T(8,128)S(1)} async-done(((f32[64,48,128]{2,1,0:T(8,128)}), f32[64,48,128]{2,1,0:T(8,128)S(1)}, u32[]{:S(2)}, u32[]{:S(2)}) %all-to-all-start.1) | async-done | bytes 1572896 | tf_op jit(solution)/shard_map/all_to_all | solution.py:38
  913.7 1.1 multiply_reduce_fusion
  916.1 0.2 reduce-precision_convert_fusion
  916.4 4.9 fusion
  921.3 0.3 fusion.17
  921.6 23.9 %psum.22 = f32[5,2048]{1,0:T(8,128)S(1)} all-reduce(f32[5,2048]{1,0:T(8,128)S(1)} %select_maximum_fusion), channel_id=1, replica_groups=mesh['samp'=64,'hour'=8] {'hour'}, use_global_device_ids=true, to_apply=%region_8.9 | all-reduce | flops 10240 | bytes 81920 | tf_op jit(solution)/shard_map/psum | solution.py:48
  945.6 0.5 slice.92
  947.0 0.6 multiply_reduce_fusion.2
  947.6 139.1 %psum.23 = f32[]{:T(128)} all-reduce(f32[]{:T(128)} %get-tuple-element.36), channel_id=1, replica_groups=mesh['samp'=64,'hour'=8] {'samp'}, use_global_device_ids=true, to_apply=%region_10.11 | all-reduce | flops 1 | bytes 8 | tf_op jit(solution)/shard_map/psum | solution.py:77
  1087.5 0.7 copy.14
  1088.2 0.6 divide_subtract_fusion.1
  (10 shorter events, 0.1 us)
Async XLA Ops:
  7.2 21.2 %copy-start = (s32[64,1024]{1,0:T(8,128)S(1)}, s32[64,1024]{1,0:T(8,128)}, u32[]{:S(2)}) copy-start(s32[64,1024]{1,0:T(8,128)} %param.11) | copy-start | bytes 786436
  8.2 20.2 %copy-start.2 = (s32[2048]{0:T(1024)S(1)}, s32[2048]{0:T(1024)}, u32[]{:S(2)}) copy-start(s32[2048]{0:T(1024)} %param.10) | copy-start | bytes 24580
  9.4 96.4 %all-to-all-start = ((f32[64,48,128]{2,1,0:T(8,128)}), f32[64,48,128]{2,1,0:T(8,128)S(1)}, u32[]{:S(2)}, u32[]{:S(2)}) async-start(f32[64,48,128]{2,1,0:T(8,128)} %stack.4), calls=%async_computation | async-start | bytes 3145728 | tf_op jit(solution)/shard_map/all_to_all | solution.py:38
  28.2 803.2 %reduce-scatter.2.cloned.1.call-start = ((), (), s32[]{:S(2)}) async-start(), calls=%async_computation.3 | async-start | bytes 1597440 | tf_op jit(solution)/shard_map/reduce_scatter | solution.py:69
  108.4 5.0 copy-start.1
  835.3 78.4 %all-to-all-start.1 = ((f32[64,48,128]{2,1,0:T(8,128)}), f32[64,48,128]{2,1,0:T(8,128)S(1)}, u32[]{:S(2)}, u32[]{:S(2)}) async-start(f32[64,48,128]{2,1,0:T(8,128)} %stack.5), calls=%async_computation.2 | async-start | bytes 3145728 | tf_op jit(solution)/shard_map/all_to_all | solution.py:38
Sparse Core Ops, SparseCore 0:
  148.0 683.2 reduce-scatter.1
